TPU v7x, 32 devices: a whole 2x2x4 slice. The times are simulated.
32 devices in a mesh: dp: 8 (over z, x), seq: 4 (over y, core).
Axes of the slice: x: 2, y: 2, z: 4, core: 2. Of those that a mesh axis runs over, the one named last changes fastest.
Arguments:
- tokens: bfloat16 [8, 1024, 768], P('dp', 'seq'), may hold values from -6 to 6
- segment_ids: int32 [8, 1024], P('dp'), may hold values from 0 to 5, never falling along the last dimension, each value on 1 to 512 neighbouring positions
- pad_lengths: int32 [8], P('dp'), may hold values from 0 to 511
- threshold: float32 [1], replicated, may hold values from 0.05 to 2
- gains: float32 [2, 768], replicated, may hold values from 0.5 to 1.5
- gain_first: float32 [2, 768], replicated, may hold values from -256 to 256
- gain_second: float32 [2, 768], replicated, may hold values from 2048 to 8192
- slot_tiles: int32 [448], replicated, may hold values from 0 to 447, as said below
- weight_slots: float32 [448, 128, 128], P(('dp', 'seq')), may hold values from -2 to 2
- first_moment: float32 [448, 128, 128], P(('dp', 'seq')), may hold values from -160 to 160
- second_moment: float32 [448, 128, 128], P(('dp', 'seq')), may hold values from 819.2 to 3276.8
- basis_left: float32 [448, 128, 128], P(('dp', 'seq')), may hold values from -1 to 1, as said below
- basis_right: float32 [448, 128, 128], P(('dp', 'seq')), may hold values from -1 to 1, as said below
- out_grad: bfloat16 [8, 1024, 768], P('dp', 'seq'), may hold values from -6 to 6
Outputs:
- output: bfloat16 [8, 1024, 768], P('dp', 'seq')
- input_grad: float32 [8, 1024, 768], P('dp', 'seq')
- fraction: float32 [8], P('dp')
- moment_first: float32 [448, 128, 128], P(('dp', 'seq'))
- moment_second: float32 [448, 128, 128], P(('dp', 'seq'))
- new_weights: float32 [448, 128, 128], P(('dp', 'seq'))
- gain_update: float32 [2, 768], replicated
- gain_moment: float32 [2, 768], replicated
- gain_square: float32 [2, 768], replicated
Inputs may be any that keep to these rules, and one draw needn't show every extreme that they name: `segment_ids`: segment numbers never fall along a row; each segment has 1 to 512 positions, one exactly that many. `slot_tiles`: a permutation of the slot numbers; a slot whose entry is 432 or more holds no tile. `basis_left`: each slot's matrix is orthogonal. `basis_right`: each slot's matrix is orthogonal.
All inputs are finite; a program needn't handle non-finite values.
Results may differ from a plain program's by a relative error of at most 0.011.
Values may be sent and summed in bfloat16 or wider, within the bound.
No kernel may reach another device: no remote copies, remote signals or barrier semaphores. Data moves between devices by JAX's collectives and lax.ppermute only.
A program may use at most 192 MiB of HBM per device.

v0:
```python
import jax
import jax.numpy as jnp
from jax import lax
from jax.sharding import PartitionSpec as P

H = 12
HD = 64
FF = 3072
STEP = 3
select_scale = 0.2
fraction_slope = 2.0
first_decay = 0.5
second_decay = 0.5
adam_epsilon = 1e-08
weight_rate = 0.05
gain_rate = 0.2
decay_rate = 0.1
norm_epsilon = 1e-05
precise = lax.Precision.HIGHEST


def carried_in(value, axis, join, neutral, backward):
    count, mine = (lax.axis_size(axis), lax.axis_index(axis))
    pieces = lax.all_gather(value, axis)
    if backward:
        pieces = pieces[::-1]
        mine = count - 1 - mine
    total = jnp.full_like(value, 0) + jnp.asarray(neutral, value.dtype)

    def step(position, total):
        longer = join(total, pieces[position])
        return jnp.where(position < mine, longer, total)

    return lax.fori_loop(0, count - 1, step, total)


def layer_norm(values, gain):
    centred = values - jnp.mean(values, axis=-1, keepdims=True)
    spread = jnp.mean(centred * centred, axis=-1, keepdims=True)
    return centred * lax.rsqrt(spread + norm_epsilon) * gain


def gelu_local(values):
    return jax.nn.gelu(values, approximate=True)


def tiles_of(matrix, tile_side):
    height, across = matrix.shape
    shaped = matrix.reshape(height // tile_side, tile_side, across // tile_side, tile_side)
    return shaped.transpose(0, 2, 1, 3).reshape(-1, tile_side, tile_side)


def matrix_of(tile_stack, height, across):
    tile_side = tile_stack.shape[-1]
    shaped = tile_stack.reshape(height // tile_side, across // tile_side, tile_side, tile_side)
    return shaped.transpose(0, 2, 1, 3).reshape(height, across)


def split_tiles(tile_stack, width, hidden_width):
    tile_side = tile_stack.shape[-1]
    shapes = [(width, 3 * width), (width, width), (width, hidden_width), (hidden_width, width)]
    result = []
    offset = 0
    for height, across in shapes:
        count_here = height * across // (tile_side * tile_side)
        result.append(matrix_of(tile_stack[offset : offset + count_here], height, across))
        offset = offset + count_here
    return result


def slot_buffer(grads, slot_tiles, tile_side, tile_count):
    stacked = jnp.concatenate(
        [tiles_of(grad, tile_side) for grad in grads]
        + [jnp.zeros((1, tile_side, tile_side), jnp.float32)],
        axis=0,
    )
    return stacked[jnp.minimum(slot_tiles, tile_count)]


def add_single(earlier, later):
    return earlier + later


def rotated_adam(grad_slots, first, second, left, right, weight, correction):
    turned = jnp.einsum("sji,sjk->sik", left, grad_slots, precision=precise)
    turned = jnp.einsum("sik,skl->sil", turned, right, precision=precise)
    first_new = first_decay * first + (1.0 - first_decay) * turned
    second_new = second_decay * second + (1.0 - second_decay) * turned * turned
    norm_step = first_new / correction / (jnp.sqrt(second_new / correction) + adam_epsilon)
    back = jnp.einsum("sik,skl->sil", left, norm_step, precision=precise)
    back = jnp.einsum("sil,sjl->sij", back, right, precision=precise)
    return (first_new, second_new, weight - weight_rate * back - weight_rate * decay_rate * weight)


def local(
    tokens,
    segment_ids,
    pad_lengths,
    threshold,
    gains,
    gain_first,
    gain_second,
    slot_tiles,
    weight_slots,
    first_moment,
    second_moment,
    basis_left,
    basis_right,
    out_grad,
):
    rows_here, tok_local, width = tokens.shape
    length = segment_ids.shape[1]
    hidden_width = FF
    heads = H
    head_dim = HD
    tile_side = weight_slots.shape[-1]
    slot_total = slot_tiles.shape[0]
    tile_count = (4 * width * width + 2 * width * hidden_width) // (tile_side * tile_side)
    query_start = lax.axis_index("seq") * tok_local
    query_pos = query_start + jnp.arange(tok_local, dtype=jnp.int32)
    key_pos = jnp.arange(length, dtype=jnp.int32)
    shared = lax.all_gather(weight_slots.astype(jnp.bfloat16), ("dp", "seq"), axis=0, tiled=True)
    tile_ids = jnp.arange(tile_count, dtype=jnp.int32)
    slot_ids = jnp.arange(slot_total, dtype=jnp.int32)
    position = jnp.sum(
        jnp.where(slot_tiles[None, :] == tile_ids[:, None], slot_ids[None, :], 0), axis=1
    )
    w_qkv, w_out, w_up, w_down = split_tiles(shared[position], width, hidden_width)
    local_ids = jnp.arange(tok_local, dtype=jnp.int32)
    lower_ones = (local_ids[None, :] < local_ids[:, None]).astype(jnp.float32)
    empty_columns = jnp.zeros((length,), jnp.float32)
    grad_sums = (
        jnp.zeros(w_qkv.shape, jnp.float32),
        jnp.zeros(w_out.shape, jnp.float32),
        jnp.zeros(w_up.shape, jnp.float32),
        jnp.zeros(w_down.shape, jnp.float32),
    )
    seg_row = segment_ids[0]
    valid_len = length - pad_lengths[0]
    seg_query = lax.dynamic_slice_in_dim(seg_row, query_start, tok_local)
    valid_keys = key_pos < valid_len
    row_input = tokens[0].astype(jnp.float32)
    normed_pre_f, pull_pre = jax.vjp(layer_norm, row_input, gains[0])
    normed_pre = normed_pre_f.astype(jnp.bfloat16)
    projected = jnp.dot(normed_pre, w_qkv, preferred_element_type=jnp.float32)
    query_heads = projected[:, :width].astype(jnp.bfloat16).reshape(tok_local, heads, head_dim)
    key_local = projected[:, width : 2 * width].astype(jnp.bfloat16)
    value_local = projected[:, 2 * width :].astype(jnp.bfloat16)
    key_all = lax.all_gather(key_local, "seq", axis=0, tiled=True)
    value_all = lax.all_gather(value_local, "seq", axis=0, tiled=True)
    key_heads = key_all.reshape(length, heads, head_dim)
    value_heads = value_all.reshape(length, heads, head_dim)
    value_float = value_heads.astype(jnp.float32)
    allowed = (seg_query[:, None] == seg_row[None, :]) & (key_pos[None, :] <= query_pos[:, None])
    allowed = allowed & (valid_keys[None, :] | (key_pos[None, :] == query_pos[:, None]))
    strict = allowed & (key_pos[None, :] < query_pos[:, None])
    strict_float = strict.astype(jnp.float32)
    allowed_float = allowed.astype(jnp.float32)
    scores = (
        jnp.einsum("qhd,khd->hqk", query_heads, key_heads, preferred_element_type=jnp.float32)
        * 0.125
    )
    select = select_scale * jax.nn.relu(scores[0]) * strict_float
    column_part = jnp.sum(select, axis=0)
    prefix = carried_in(column_part, "seq", add_single, empty_columns, False)
    shadow = prefix[None, :] + jnp.dot(lower_ones, select, precision=precise)
    logits = jnp.where(allowed[None], scores - shadow[None], -1e30)
    row_max = jnp.max(logits, axis=2)
    exps = jnp.exp(logits - row_max[:, :, None]) * allowed_float[None]
    totals = jnp.sum(exps, axis=2)
    probs = exps / totals[:, :, None]
    mixed_out = jnp.einsum("hqk,khd->qhd", probs, value_float, precision=precise).reshape(
        tok_local, width
    )
    column_total = lax.psum(column_part, "seq")
    counted = jnp.sum(
        valid_keys.astype(jnp.float32)
        * jax.nn.sigmoid((column_total - threshold[0]) * fraction_slope)
    )
    fraction_rows = [counted / valid_len.astype(jnp.float32)]
    mixed_b = mixed_out.astype(jnp.bfloat16)
    hidden_one = row_input + jnp.dot(mixed_b, w_out, preferred_element_type=jnp.float32)
    normed_mid_f, pull_mid = jax.vjp(layer_norm, hidden_one, gains[1])
    normed_mid = normed_mid_f.astype(jnp.bfloat16)
    upper = jnp.dot(normed_mid, w_up, preferred_element_type=jnp.float32)
    active_f, pull_gelu = jax.vjp(gelu_local, upper)
    active = active_f.astype(jnp.bfloat16)
    result = hidden_one + jnp.dot(active, w_down, preferred_element_type=jnp.float32)
    output_rows = [result.astype(jnp.bfloat16)]
    row_grad = out_grad[0]
    grad_down = jnp.einsum("tf,td->fd", active, row_grad, preferred_element_type=jnp.float32)
    grad_active = jnp.einsum("td,fd->tf", row_grad, w_down, preferred_element_type=jnp.float32)
    grad_upper = pull_gelu(grad_active)[0].astype(jnp.bfloat16)
    grad_up = jnp.einsum("td,tf->df", normed_mid, grad_upper, preferred_element_type=jnp.float32)
    grad_mid = jnp.einsum("tf,df->td", grad_upper, w_up, preferred_element_type=jnp.float32)
    grad_hidden_ln, grad_gain_mid = pull_mid(grad_mid)
    grad_hidden = row_grad.astype(jnp.float32) + grad_hidden_ln
    grad_branch = grad_hidden.astype(jnp.bfloat16)
    grad_out = jnp.einsum("td,te->de", mixed_b, grad_branch, preferred_element_type=jnp.float32)
    grad_mixed = jnp.einsum(
        "te,de->td", grad_branch, w_out, preferred_element_type=jnp.float32
    ).astype(jnp.bfloat16)
    delta_rows = jnp.sum(
        (grad_mixed.astype(jnp.float32) * mixed_out).reshape(tok_local, heads, head_dim), axis=2
    )
    grad_heads = grad_mixed.reshape(tok_local, heads, head_dim)
    dprob = jnp.einsum("qhd,khd->hqk", grad_heads, value_heads, preferred_element_type=jnp.float32)
    grad_values_part = jnp.einsum(
        "hqk,qhd->khd", probs, grad_heads.astype(jnp.float32), precision=precise
    )
    dlogit = probs * (dprob - delta_rows.T[:, :, None])
    grad_shadow = -jnp.sum(dlogit, axis=0)
    shadow_columns = jnp.sum(grad_shadow, axis=0)
    suffix = carried_in(shadow_columns, "seq", add_single, empty_columns, True)
    grad_select = jnp.dot(lower_ones.T, grad_shadow, precision=precise) + suffix[None, :]
    head_zero = (
        dlogit[0]
        + grad_select * select_scale * (scores[0] > 0.0).astype(jnp.float32) * strict_float
    )
    grad_scores = jnp.concatenate([head_zero[None], dlogit[1:]], axis=0).astype(jnp.bfloat16)
    grad_query = (
        jnp.einsum("hqk,khd->qhd", grad_scores, key_heads, preferred_element_type=jnp.float32)
        * 0.125
    ).reshape(tok_local, width)
    grad_keys_part = (
        jnp.einsum("hqk,qhd->khd", grad_scores, query_heads, preferred_element_type=jnp.float32)
        * 0.125
    )
    grad_keys = lax.psum_scatter(
        grad_keys_part.reshape(length, width).astype(jnp.bfloat16),
        "seq",
        scatter_dimension=0,
        tiled=True,
    )
    grad_values = lax.psum_scatter(
        grad_values_part.reshape(length, width).astype(jnp.bfloat16),
        "seq",
        scatter_dimension=0,
        tiled=True,
    )
    grad_qkv = jnp.concatenate([grad_query.astype(jnp.bfloat16), grad_keys, grad_values], axis=1)
    grad_qkv_w = jnp.einsum("td,te->de", normed_pre, grad_qkv, preferred_element_type=jnp.float32)
    grad_pre = jnp.einsum("te,de->td", grad_qkv, w_qkv, preferred_element_type=jnp.float32)
    grad_input_ln, grad_gain_pre = pull_pre(grad_pre)
    input_rows = [grad_hidden + grad_input_ln]
    gain_grad = jnp.stack([grad_gain_pre, grad_gain_mid])
    grad_sums = (grad_qkv_w, grad_out, grad_up, grad_down)
    owned_grad = lax.psum_scatter(
        slot_buffer(grad_sums, slot_tiles, tile_side, tile_count),
        ("dp", "seq"),
        scatter_dimension=0,
        tiled=True,
    )
    gain_total = lax.psum(gain_grad, ("dp", "seq"))
    correction = 1.0 - first_decay**STEP
    moment_first, moment_second, new_weights = rotated_adam(
        owned_grad, first_moment, second_moment, basis_left, basis_right, weight_slots, correction
    )
    gain_moment = first_decay * gain_first + (1.0 - first_decay) * gain_total
    gain_square = second_decay * gain_second + (1.0 - second_decay) * gain_total * gain_total
    gain_update = gains - gain_rate * (gain_moment / correction) / (
        jnp.sqrt(gain_square / correction) + adam_epsilon
    )
    return (
        jnp.stack(output_rows),
        jnp.stack(input_rows),
        jnp.stack(fraction_rows),
        moment_first,
        moment_second,
        new_weights,
        gain_update,
        gain_moment,
        gain_square,
    )


def solution(mesh):
    in_specs = (
        P("dp", "seq", None),
        P("dp", None),
        P("dp"),
        P(),
        P(),
        P(),
        P(),
        P(),
        P(("dp", "seq"), None, None),
        P(("dp", "seq"), None, None),
        P(("dp", "seq"), None, None),
        P(("dp", "seq"), None, None),
        P(("dp", "seq"), None, None),
        P("dp", "seq", None),
    )
    out_specs = (
        P("dp", "seq", None),
        P("dp", "seq", None),
        P("dp"),
        P(("dp", "seq"), None, None),
        P(("dp", "seq"), None, None),
        P(("dp", "seq"), None, None),
        P(),
        P(),
        P(),
    )
    return jax.shard_map(local, mesh=mesh, in_specs=in_specs, out_specs=out_specs, check_vma=False)
```

profile of v0, /device:TPU:1, one launch (start us, length us, event | category | flops | bytes accessed | tf_op | source)
XLA Modules:
  0.0 714.0 jit_solution(11046674508676594106)
XLA Ops:
  7.2 2.1 convert_element_type.104
  14.0 105.3 %all-gather.6.cloned.1.call-done = bf16[448,128,128]{2,1,0:T(8,128)(2,1)} async-done(((bf16[14,128,128]{2,1,0:T(8,128)(2,1)}), bf16[448,128,128]{2,1,0:T(8,128)(2,1)}) %all-gather.6.cloned.1.call-update) | async-done | bytes 14680080 | tf_op jit(solution)/shard_map/all_gather | solution.py:122
  119.3 18.3 %gather_fusion = bf16[432,128,128]{2,1,0:T(8,128)(2,1)} fusion(bf16[448,128,128]{2,1,0:T(8,128)(2,1)} %all-gather.6.cloned.1.call-done, s32[1024]{0:T(1024)S(1)} %pad_clamp_fusion.1), kind=kCustom, calls=%fused_computation | custom fusion | bytes 28313280 | tf_op jit(solution)/shard_map/gather | solution.py:128
  137.6 2.0 slice-done
  139.6 2.4 copy.73
  148.1 2.0 copy.77
  150.1 12.0 %fusion.132 = (bf16[144,128,128]{2,1,0:T(8,128)(2,1)}, bf16[144,128,128]{2,1,0:T(8,128)(2,1)}) fusion(bf16[432,128,128]{2,1,0:T(8,128)(2,1)} %gather_fusion), kind=kLoop, calls=%fused_computation.197 | loop fusion | bytes 18874368 | tf_op jit(solution)/shard_map/slice | solution.py:66
  162.1 6.9 copy.79
  169.0 7.5 %copy.78 = bf16[6,24,128,128]{3,1,2,0:T(8,128)(2,1)} copy(bf16[6,24,128,128]{3,2,1,0:T(8,128)(2,1)} %bitcast.240) | data formatting | bytes 9437184 | tf_op jit(solution)/shard_map/reshape | solution.py:55
  178.4 1.8 broadcast_multiply_fusion
  180.3 4.7 copy-done.1
  186.2 5.5 all-gather
  192.0 2.6 convolution_add_fusion.1
  194.6 17.9 %fusion.134 = (f32[12,256]{1,0:T(8,128)S(1)}, f32[12,256,1024]{2,1,0:T(8,128)}) fusion(f32[256,1024]{1,0:T(8,128)S(1)} %copy-done.31, f32[12,256,1024]{2,1,0:T(8,128)} %copy-done.1, f32[256,1024]{1,0:T(8,128)S(1)} %convolution_add_fusion.1, pred[256,1024]{1,0:T(8,128)(4,1)S(1)} %get-tuple-element.238), kind=kOutput, calls=%fused_computation.199 | output fusion | flops 22021120 | bytes 27537408 | tf_op jit(solution)/shard_map/sub | solution.py:169
  212.5 1.7 copy.74
  214.3 10.6 %fusion.128 = f32[12,64,256]{2,1,0:T(8,128)S(1)} fusion(bf16[1024,12,64]{0,2,1:T(8,128)(2,1)S(1)} %bitcast.266, f32[12,256,1024]{2,1,0:T(8,128)} %get-tuple-element.241, f32[12,256]{1,0:T(8,128)S(1)} %get-tuple-element.240), kind=kOutput, calls=%fused_computation.194 | convolution fusion | flops 2419064832 | bytes 14954496 | tf_op jit(solution)/shard_map/hqk,khd->qhd/dot_general | solution.py:172
  226.7 3.3 fusion.39
  230.1 3.8 fusion.31
  233.9 2.3 multiply_reduce_fusion
  236.3 2.4 copy.82
  245.0 11.4 %convolution_convert_fusion.1 = bf16[12,64,1024]{2,1,0:T(8,128)(2,1)} fusion(bf16[256,12,64]{0,2,1:T(8,128)(2,1)S(1)} %bitcast.277, f32[12,256,1024]{2,1,0:T(8,128)} %get-tuple-element.241, f32[12,256]{1,0:T(8,128)S(1)} %copy-done.64), kind=kOutput, calls=%fused_computation.60 | convolution fusion | flops 2419851264 | bytes 14561280 | tf_op jit(solution)/shard_map/hqk,qhd->khd/dot_general | solution.py:208
  256.8 11.6 %fusion.129 = (f32[1024]{0:T(1024)S(1)}, f32[256,1024]{1,0:T(8,128)}, f32[12,256,1024]{2,1,0:T(8,128)}) fusion(f32[12,256]{1,0:T(8,128)S(1)} %bitcast.284, bf16[256,12,64]{0,2,1:T(8,128)(2,1)} %bitcast.278, bf16[1024,12,64]{0,2,1:T(8,128)(2,1)} %bitcast.267, f32[12,256,1024]{2,1,0:T(8,128)} %get-tuple-element.241, f32[12,256]{1,0:T(8,128)S(1)} %copy-done.64), kind=kOutput, calls=%fused_computation.195 | convolution fusion | flops 418118656 | bytes 28209152 | tf_op jit(solution)/shard_map/qhd,khd->hqk/dot_general | solution.py:207
  268.4 8.0 %slice.78 = bf16[11,256,1024]{2,1,0:T(8,128)(2,1)} slice(f32[12,256,1024]{2,1,0:T(8,128)} %get-tuple-element.247), slice={[1:12], [0:256], [0:1024]} | slice | bytes 11534336 | tf_op jit(solution)/shard_map/slice | solution.py:220
  276.5 5.3 all-gather.1
  282.2 3.2 fusion.63
  285.5 5.2 multiply_convert_fusion
  292.6 3.0 convolution_bitcast_fusion
  295.6 5.8 copy.106
  301.4 9.1 %copy.86 = f32[6,128,24,128]{3,1,2,0:T(8,128)} copy(f32[6,128,24,128]{3,2,1,0:T(8,128)} %bitcast.238) | data formatting | bytes 18874368 | tf_op jit(solution)/shard_map/reshape | solution.py:49
  310.5 1.8 copy.101
  312.2 1.8 fusion.137
  314.0 5.6 fusion.62
  319.6 4.7 fusion.138
  324.3 4.0 fusion.93
  329.5 1.9 copy.84
  332.7 2.1 fusion.136
  334.9 4.1 constant_dynamic-update-slice_fusion.3
  341.9 4.4 constant_dynamic-update-slice_fusion.1
  346.3 8.6 %constant_dynamic-update-slice_fusion = f32[433,128,128]{2,1,0:T(8,128)} fusion(f32[433,128,128]{2,1,0:T(8,128)} %constant_dynamic-update-slice_fusion.1, f32[144,128,128]{2,1,0:T(8,128)} %bitcast.237), kind=kLoop, calls=%fused_computation.152 | loop fusion | bytes 18874368
  355.5 26.1 %gather_fusion.1 = f32[448,128,128]{2,1,0:T(8,128)} fusion(f32[433,128,128]{2,1,0:T(8,128)} %broadcast_dynamic-update-slice_fusion, s32[1024]{0:T(1024)S(1)} %pad_clamp_fusion), kind=kCustom, calls=%fused_computation.1 | custom fusion | bytes 58722048 | tf_op jit(solution)/shard_map/gather | solution.py:77
  382.3 5.5 psum.14
  389.2 6.4 fusion.64
  395.6 57.1 %psum.15 = f32[2,768]{1,0:T(2,128)S(1)} all-reduce(f32[2,768]{1,0:T(2,128)S(1)} %pad_maximum_fusion.10), channel_id=1, replica_groups=mesh['dp'=8,'seq'=4] {'dp','seq'}, use_global_device_ids=true, to_apply=%region_26.27 | all-reduce | flops 1536 | bytes 12288 | tf_op jit(solution)/shard_map/psum | solution.py:254
  453.3 2.4 add_bitcast_fusion
  455.7 239.3 %reduce-scatter.8.cloned.1.call-done = f32[14,128,128]{2,1,0:T(8,128)} async-done(((f32[448,128,128]{2,1,0:T(8,128)}), f32[14,128,128]{2,1,0:T(8,128)}) %reduce-scatter.8.cloned.1.call-update) | async-done | bytes 917520 | tf_op jit(solution)/shard_map/reduce_scatter | solution.py:248
  695.1 3.1 fusion.139
  698.2 2.8 fusion.79
  702.8 3.0 fusion.53
  (231 shorter events, 33.4 us)
Async XLA Ops:
  7.2 691.0 %copy-start = (f32[14,128,128]{2,1,0:T(8,128)S(1)}, f32[14,128,128]{2,1,0:T(8,128)}, u32[]{:S(2)}) copy-start(f32[14,128,128]{2,1,0:T(8,128)} %param.30) | copy-start | bytes 2752516
  7.2 112.1 %all-gather.6.cloned.1.call-start = ((), (), s32[]{:S(2)}) async-start(), calls=%async_computation.3 | async-start | bytes 15138816 | tf_op jit(solution)/shard_map/all_gather | solution.py:122
  9.4 167.3 %all-gather.10.cloned.1.call-start = ((), (), s32[]{:S(2)}) async-start(), calls=%async_computation.5 | async-start | bytes 1966080 | tf_op jit(solution)/shard_map/all_gather | solution.py:149
  12.2 129.8 %copy-start.42 = (f32[256]{0:T(256)}, f32[256]{0:T(256)S(1)}, u32[]{:S(2)}) copy-start(f32[256]{0:T(256)S(1)} %broadcast_multiply_fusion.2) | copy-start | bytes 3076
  14.0 128.0 %copy-start.44 = (f32[256]{0:T(256)}, f32[256]{0:T(256)S(1)}, u32[]{:S(2)}) copy-start(f32[256]{0:T(256)S(1)} %fusion.112) | copy-start | bytes 3076
  145.2 67.3 %all-gather.8.cloned.1.call-start = ((), (), s32[]{:S(2)}) async-start(), calls=%async_computation.4 | async-start | bytes 1966080 | tf_op jit(solution)/shard_map/all_gather | solution.py:150
  148.1 30.2 %copy-start.29 = (bf16[256,768]{0,1:T(8,128)(2,1)}, bf16[256,768]{0,1:T(8,128)(2,1)S(1)}, u32[]{:S(2)}) copy-start(bf16[256,768]{0,1:T(8,128)(2,1)S(1)} %copy.75) | copy-start | bytes 1179652
  176.6 147.7 %reduce-scatter.6.cloned.1.call-start = ((), (), s32[]{:S(2)}) async-start(), calls=%async_computation.7 | async-start | bytes 1966080 | tf_op jit(solution)/shard_map/reduce_scatter | solution.py:235
  178.4 6.6 copy-start.40
  178.4 6.5 copy-start.49
  178.4 6.5 copy-start.55
  178.4 6.5 copy-start.58
  186.2 8.4 %copy-start.31 = (f32[256,1024]{1,0:T(8,128)S(1)}, f32[256,1024]{1,0:T(8,128)}, u32[]{:S(2)}) copy-start(f32[256,1024]{1,0:T(8,128)} %get-tuple-element.239) | copy-start | bytes 3145732
  212.5 12.4 %copy-start.63 = (f32[12,256]{1,0:T(8,128)}, f32[12,256]{1,0:T(8,128)S(1)}, u32[]{:S(2)}) copy-start(f32[12,256]{1,0:T(8,128)S(1)} %get-tuple-element.240) | copy-start | bytes 36868
  214.2 10.7 %copy-start.27 = (bf16[1024,768]{0,1:T(8,128)(2,1)}, bf16[1024,768]{0,1:T(8,128)(2,1)S(1)}, u32[]{:S(2)}) copy-start(bf16[1024,768]{0,1:T(8,128)(2,1)S(1)} %copy.74) | copy-start | bytes 4718596
  214.2 12.4 %slice-start.7 = ((s8[4718592]{0:T(1024)(128)(4,1)}), s8[4194304]{0:T(1024)(128)(4,1)S(1)}, s32[]{:S(2)}) async-start(s8[4718592]{0:T(1024)(128)(4,1)} %bitcast.252), calls=%async_computation.16 | async-start | bytes 8388608
  214.3 11.6 %copy-start.12 = (bf16[6,6,128,128]{3,1,2,0:T(8,128)(2,1)S(1)}, bf16[6,6,128,128]{3,1,2,0:T(8,128)(2,1)}, u32[]{:S(2)}) copy-start(bf16[6,6,128,128]{3,1,2,0:T(8,128)(2,1)} %copy.77) | copy-start | bytes 3538948
  214.3 12.4 %slice-start.8 = ((s8[4718592]{0:T(1024)(128)(4,1)}), s8[524288]{0:T(1024)(128)(4,1)S(1)}, s32[]{:S(2)}) async-start(s8[4718592]{0:T(1024)(128)(4,1)} %bitcast.252), calls=%async_computation.17 | async-start | bytes 1048576
  225.0 5.1 copy-start.23
  226.4 66.2 %copy-start.4 = (f32[256,768]{1,0:T(8,128)}, f32[256,768]{1,0:T(8,128)S(1)}, u32[]{:S(2)}) copy-start(f32[256,768]{1,0:T(8,128)S(1)} %get-tuple-element.243) | copy-start | bytes 2359300
  236.3 6.0 copy-start.13
  245.0 11.4 %copy-start.35 = (bf16[256,768]{0,1:T(8,128)(2,1)}, bf16[256,768]{0,1:T(8,128)(2,1)S(1)}, u32[]{:S(2)}) copy-start(bf16[256,768]{0,1:T(8,128)(2,1)S(1)} %copy.81) | copy-start | bytes 1179652
  245.0 11.5 %copy-start.21 = (f32[256,768]{1,0:T(8,128)S(1)}, f32[256,768]{1,0:T(8,128)}, u32[]{:S(2)}) copy-start(f32[256,768]{1,0:T(8,128)} %get-tuple-element.245) | copy-start | bytes 2359300
  256.4 67.8 %reduce-scatter.4.cloned.1.call-start = ((), (), s32[]{:S(2)}) async-start(), calls=%async_computation.6 | async-start | bytes 1966080 | tf_op jit(solution)/shard_map/reduce_scatter | solution.py:229
  268.4 13.8 %copy-start.41 = (s32[1,1024]{1,0:T(1,128)S(1)}, s32[1,1024]{1,0:T(1,128)}, u32[]{:S(2)}) copy-start(s32[1,1024]{1,0:T(1,128)} %param.19) | copy-start | bytes 12292
  268.4 13.8 %copy-start.50 = (s32[1,256]{1,0:T(1,128)S(1)}, s32[1,256]{1,0:T(1,128)}, u32[]{:S(2)}) copy-start(s32[1,256]{1,0:T(1,128)} %copy-done.48) | copy-start | bytes 3076
  268.4 13.8 %copy-start.56 = (s32[256]{0:T(256)S(1)}, s32[256]{0:T(256)}, u32[]{:S(2)}) copy-start(s32[256]{0:T(256)} %copy-done.54) | copy-start | bytes 3076
  268.4 13.8 %copy-start.59 = (pred[1024]{0:T(1024)(128)(4,1)S(1)}, pred[1024]{0:T(1024)(128)(4,1)}, u32[]{:S(2)}) copy-start(pred[1024]{0:T(1024)(128)(4,1)} %copy-done.57) | copy-start | bytes 3076
  276.5 9.0 %copy-start.30 = (bf16[256,768]{0,1:T(8,128)(2,1)S(1)}, bf16[256,768]{0,1:T(8,128)(2,1)}, u32[]{:S(2)}) copy-start(bf16[256,768]{0,1:T(8,128)(2,1)} %copy-done.29) | copy-start | bytes 1179652
  285.5 5.2 copy-start.60
  285.5 5.3 copy-start.19
  285.5 6.2 copy-start.51
  285.5 6.2 copy-start.17
  290.7 404.4 %reduce-scatter.8.cloned.1.call-start = ((), (), s32[]{:S(2)}) async-start(), calls=%async_computation.8 | async-start | bytes 30277632 | tf_op jit(solution)/shard_map/reduce_scatter | solution.py:248
  301.4 9.1 %copy-start.26 = (bf16[3072,256]{0,1:T(8,128)(2,1)S(1)}, bf16[3072,256]{0,1:T(8,128)(2,1)}, u32[]{:S(2)}) copy-start(bf16[3072,256]{0,1:T(8,128)(2,1)} %get-tuple-element.250) | copy-start | bytes 4718596
  314.0 5.6 copy-start.11
  314.0 5.6 copy-start.25
  334.8 5.7 slice-start.2
  334.8 6.9 slice-start.3
  334.9 7.1 slice-start.4
  381.5 7.5 %copy-start.5 = (f32[256,768]{1,0:T(8,128)S(1)}, f32[256,768]{1,0:T(8,128)}, u32[]{:S(2)}) copy-start(f32[256,768]{1,0:T(8,128)} %copy-done.4) | copy-start | bytes 2359300
  389.1 63.6 %copy-start.38 = (f32[2,768]{1,0:T(2,128)S(1)}, f32[2,768]{1,0:T(2,128)}, u32[]{:S(2)}) copy-start(f32[2,768]{1,0:T(2,128)} %param.22) | copy-start | bytes 18436
  389.1 63.6 %copy-start.52 = (f32[2,768]{1,0:T(2,128)S(1)}, f32[2,768]{1,0:T(2,128)}, u32[]{:S(2)}) copy-start(f32[2,768]{1,0:T(2,128)} %param.23) | copy-start | bytes 18436
  389.1 63.6 %copy-start.53 = (f32[2,768]{1,0:T(2,128)S(1)}, f32[2,768]{1,0:T(2,128)}, u32[]{:S(2)}) copy-start(f32[2,768]{1,0:T(2,128)} %param.24) | copy-start | bytes 18436
  389.1 64.2 %copy-start.3 = (f32[256,768]{1,0:T(8,128)S(1)}, f32[256,768]{1,0:T(8,128)}, u32[]{:S(2)}) copy-start(f32[256,768]{1,0:T(8,128)} %copy-done.2) | copy-start | bytes 2359300
  389.1 64.2 %copy-start.10 = (bf16[1,256,768]{2,1,0:T(8,128)(2,1)S(1)}, bf16[1,256,768]{2,1,0:T(8,128)(2,1)}, u32[]{:S(2)}) copy-start(bf16[1,256,768]{2,1,0:T(8,128)(2,1)} %param.18) | copy-start | bytes 1179652
  389.1 64.2 %copy-start.20 = (bf16[1,256,768]{2,1,0:T(8,128)(2,1)S(1)}, bf16[1,256,768]{2,1,0:T(8,128)(2,1)}, u32[]{:S(2)}) copy-start(bf16[1,256,768]{2,1,0:T(8,128)(2,1)} %param.31) | copy-start | bytes 1179652
  701.0 4.8 copy-start.33
  (32 other events, 87.0 us)
Sparse Core Ops, SparseCore 0:
  11.4 107.8 all-gather.5
  145.3 17.7 all-gather.9
  176.7 18.1 all-gather.7
  256.6 26.2 reduce-scatter.5
  290.8 25.6 reduce-scatter.3
  381.7 313.3 reduce-scatter.7
where the time goes:
time: 721 us; the launch traced here: 714 us
  waiting for transfers between devices  345 us (48%)
  local copies, waits for them, and re-layouts  144 us (20%)
  matrix products  97 us (13%)
  blocking collectives  73.4 us (10%)
  other arithmetic  35.5 us (5%)
  between operations  18.5 us (3%)
    reduce_scatter x1, waiting for transfers between devices, local(): lax.psum_scatter(slot_buffer(grad_sums, slot_tiles, tile_side, tile_count...  239 us
    all_gather x1, waiting for transfers between devices, local(): lax.all_gather(weight_slots.astype(jnp.bfloat16), ('dp', 'seq'), axis=0,...  105 us
    psum x1, blocking collectives, local(): gain_total = lax.psum(gain_grad, ('dp', 'seq'))  57.1 us
    unnamed x149, local copies, waits for them, and re-layouts  34 us
    gather x1, local copies, waits for them, and re-layouts, slot_buffer(): return stacked[jnp.minimum(slot_tiles, tile_count)]  26.1 us
    reshape x4, local copies, waits for them, and re-layouts, matrix_of(): tile_stack.reshape(height // tile_side, across // tile_side, tile_side, t...  18.8 us
    gather x1, local copies, waits for them, and re-layouts, local(): shared[position]  18.3 us
    sub x1, other arithmetic, local(): exps = jnp.exp(logits - row_max[:, :, None]) * allowed_float[None]  17.9 us
  transfers between devices with their start and end apart: 6, of which 2 were waited for; matrix products, arithmetic and copies ran while one was open for 18% of the time, Pallas kernels for 0%

commit v1 on v0

--- a/solution.py
+++ b/solution.py
@@ -17,6 +17,35 @@
 decay_rate = 0.1
 norm_epsilon = 1e-05
 precise = lax.Precision.HIGHEST
+
+
+def _draft_stacks_all(xin, array_axis):
+    parts_out = list(xin.shape[1:])
+    parts_out[array_axis] *= xin.shape[0]
+    all_rows = jnp.moveaxis(xin, 0, array_axis).reshape(parts_out)
+    return all_rows
+
+
+def rates_pass(mat, row_axis):
+    k_all = jax.lax.axis_size(row_axis)
+    odd = mat[None]
+    for dev in range(k_all.bit_length() - 1):
+        frame_out = 1 << dev
+        line_up = []
+        k0 = 0
+        while k0 < k_all:
+            line_up.append((k0, k0 ^ frame_out))
+            k0 += 1
+        n_now = jax.lax.ppermute(odd, axis_name=row_axis, perm=line_up)
+        long_array = jnp.stack([odd, n_now], axis=0)
+        g_now = jax.lax.axis_index(row_axis) >> dev & 1
+        odd = jnp.where(g_now == 0, long_array, long_array[::-1]).reshape(-1, *mat.shape)
+    return odd
+
+
+def screen_change(point, shard_in, which_dim=0):
+    val2 = _draft_stacks_all(rates_pass(point, shard_in), which_dim)
+    return val2
 
 
 def carried_in(value, axis, join, neutral, backward):
@@ -119,7 +148,7 @@
     query_start = lax.axis_index("seq") * tok_local
     query_pos = query_start + jnp.arange(tok_local, dtype=jnp.int32)
     key_pos = jnp.arange(length, dtype=jnp.int32)
-    shared = lax.all_gather(weight_slots.astype(jnp.bfloat16), ("dp", "seq"), axis=0, tiled=True)
+    shared = screen_change(weight_slots.astype(jnp.bfloat16), ("dp", "seq"))
     tile_ids = jnp.arange(tile_count, dtype=jnp.int32)
     slot_ids = jnp.arange(slot_total, dtype=jnp.int32)
     position = jnp.sum(

time: 721 us -> 1110 us (1.54)
  waiting for transfers between devices: 345 us -> 707 us
  other arithmetic: 35.5 us -> 64.7 us
    ppermute x0 -> x5, waiting for transfers between devices: none -> 456 us  [rates_pass(): n_now = jax.lax.ppermute(odd, axis_name=row_axis, perm=line_up)]
    all_gather x1 -> x0, waiting for transfers between devices: 105 us -> none  [local(): lax.all_gather(weight_slots.astype(jnp.bfloat16), ('dp', 'seq'), axis=0,...]
    transpose x0 -> x4, local copies, waits for them, and re-layouts: none -> 19.4 us  [matrix_of(): return shaped.transpose(0, 2, 1, 3).reshape(height, across)]
    reshape x4 -> x0, local copies, waits for them, and re-layouts: 18.8 us -> none  [matrix_of(): tile_stack.reshape(height // tile_side, across // tile_side, tile_side, t...]
    select_n x0 -> x4, other arithmetic: none -> 17 us  [rates_pass(): jnp.where(g_now == 0, long_array, long_array[::-1]).reshape(-1, *mat.shape)]
    another operation x0 -> x7, other arithmetic: none -> 16.4 us  [rates_pass(): long_array = jnp.stack([odd, n_now], axis=0)]
    reduce_scatter x1, waiting for transfers between devices: 239 us -> 251 us  [local(): lax.psum_scatter(slot_buffer(grad_sums, slot_tiles, tile_side, tile_count...]
  transfers between devices with their start and end apart: 6 -> 10, of which waited for: 2 -> 6; matrix products, arithmetic and copies ran while one was open for 18% -> 12% of each run, Pallas kernels for 0% -> 0%
where the time goes in v1:
time: 1110 us; the launch traced here: 1100 us
  waiting for transfers between devices  707 us (64%)
  local copies, waits for them, and re-layouts  143 us (13%)
  matrix products  97 us (9%)
  other arithmetic  64.7 us (6%)
  blocking collectives  64.5 us (6%)
  between operations  18.3 us (2%)
    ppermute x5, waiting for transfers between devices, rates_pass(): n_now = jax.lax.ppermute(odd, axis_name=row_axis, perm=line_up)  456 us
    reduce_scatter x1, waiting for transfers between devices, local(): lax.psum_scatter(slot_buffer(grad_sums, slot_tiles, tile_side, tile_count...  251 us
    psum x1, blocking collectives, local(): gain_total = lax.psum(gain_grad, ('dp', 'seq'))  47.8 us
    unnamed x149, local copies, waits for them, and re-layouts  33.1 us
    gather x1, local copies, waits for them, and re-layouts, slot_buffer(): return stacked[jnp.minimum(slot_tiles, tile_count)]  26.1 us
  transfers between devices with their start and end apart: 10, of which 6 were waited for; matrix products, arithmetic and copies ran while one was open for 12% of the time, Pallas kernels for 0%

profile of v1, /device:TPU:1, one launch (start us, length us, event | category | flops | bytes accessed | tf_op | source)
XLA Modules:
  0.0 1100.7 jit_solution(9216307372026073719)
XLA Ops:
  12.0 2.4 collective-permute-start.1
  14.4 20.6 %collective-permute-done.1 = bf16[2,14,128,128]{3,2,1,0:T(8,128)(2,1)S(1)} collective-permute-done((bf16[2,14,128,128]{3,2,1,0:T(8,128)(2,1)}, bf16[2,14,128,128]{3,2,1,0:T(8,128)(2,1)S(1)}, u32[]{:S(2)}, u32[]{:S(2)}) %collective-permute-start.1) | collective-permute-done | bytes 917536 | tf_op jit(solution)/shard_map/ppermute | solution.py:39
  36.9 39.6 %collective-permute-done.2 = bf16[4,14,128,128]{3,2,1,0:T(8,128)(2,1)} collective-permute-done((bf16[4,14,128,128]{3,2,1,0:T(8,128)(2,1)S(1)}, bf16[4,14,128,128]{3,2,1,0:T(8,128)(2,1)}, u32[]{:S(2)}, u32[]{:S(2)}) %collective-permute-start.2) | collective-permute-done | bytes 1835040 | tf_op jit(solution)/shard_map/ppermute | solution.py:39
  78.4 2.8 reverse_select_fusion.2
  82.1 78.5 %collective-permute-done.3 = bf16[8,14,128,128]{3,2,1,0:T(8,128)(2,1)} collective-permute-done((bf16[8,14,128,128]{3,2,1,0:T(8,128)(2,1)}, bf16[8,14,128,128]{3,2,1,0:T(8,128)(2,1)}, u32[]{:S(2)}, u32[]{:S(2)}) %collective-permute-start.3) | collective-permute-done | bytes 3670048 | tf_op jit(solution)/shard_map/ppermute | solution.py:39
  160.6 3.8 pad_maximum_fusion.1
  164.4 6.2 reverse_select_fusion.1
  173.5 315.4 %collective-permute-done.4 = bf16[16,14,128,128]{3,2,1,0:T(8,128)(2,1)} collective-permute-done((bf16[16,14,128,128]{3,2,1,0:T(8,128)(2,1)}, bf16[16,14,128,128]{3,2,1,0:T(8,128)(2,1)}, u32[]{:S(2)}, u32[]{:S(2)}) %collective-permute-start.4) | collective-permute-done | bytes 7340064 | tf_op jit(solution)/shard_map/ppermute | solution.py:39
  488.8 7.6 pad_maximum_fusion
  496.5 7.4 reverse_select_fusion
  503.9 18.3 %gather_fusion = bf16[432,128,128]{2,1,0:T(8,128)(2,1)} fusion(bf16[448,128,128]{2,1,0:T(8,128)(2,1)} %bitcast.256, s32[1024]{0:T(1024)S(1)} %get-tuple-element.257), kind=kCustom, calls=%fused_computation | custom fusion | bytes 28313280 | tf_op jit(solution)/shard_map/gather | solution.py:157
  524.2 2.4 copy.89
  534.2 11.9 %fusion.134 = (bf16[144,128,128]{2,1,0:T(8,128)(2,1)}, bf16[144,128,128]{2,1,0:T(8,128)(2,1)}) fusion(bf16[432,128,128]{2,1,0:T(8,128)(2,1)} %gather_fusion), kind=kLoop, calls=%fused_computation.211 | loop fusion | bytes 18874368 | tf_op jit(solution)/shard_map/slice | solution.py:95
  546.2 7.4 copy.95
  553.6 7.5 copy.94
  564.8 4.6 copy-done.1
  570.7 6.0 all-gather
  577.1 2.6 convolution_add_fusion.1
  579.8 18.0 %fusion.136 = (f32[12,256]{1,0:T(8,128)S(1)}, f32[12,256,1024]{2,1,0:T(8,128)}) fusion(f32[256,1024]{1,0:T(8,128)S(1)} %copy-done.30, f32[12,256,1024]{2,1,0:T(8,128)} %copy-done.1, f32[256,1024]{1,0:T(8,128)S(1)} %convolution_add_fusion.1, pred[256,1024]{1,0:T(8,128)(4,1)S(1)} %get-tuple-element.242), kind=kOutput, calls=%fused_computation.213 | output fusion | flops 22021120 | bytes 27537408 | tf_op jit(solution)/shard_map/sub | solution.py:198
  599.5 10.6 fusion.130
  612.0 3.3 fusion.39
  615.3 3.8 fusion.31
  619.2 2.3 multiply_reduce_fusion
  621.5 2.4 copy.98
  630.3 11.4 %convolution_convert_fusion.1 = bf16[12,64,1024]{2,1,0:T(8,128)(2,1)} fusion(bf16[256,12,64]{0,2,1:T(8,128)(2,1)S(1)} %bitcast.306, f32[12,256,1024]{2,1,0:T(8,128)} %get-tuple-element.245, f32[12,256]{1,0:T(8,128)S(1)} %copy-done.64), kind=kOutput, calls=%fused_computation.68 | convolution fusion | flops 2419851264 | bytes 14561280 | tf_op jit(solution)/shard_map/hqk,qhd->khd/dot_general | solution.py:237
  642.1 11.3 %fusion.131 = (f32[1024]{0:T(1024)S(1)}, f32[256,1024]{1,0:T(8,128)}, f32[12,256,1024]{2,1,0:T(8,128)}) fusion(f32[12,256]{1,0:T(8,128)S(1)} %bitcast.313, bf16[256,12,64]{0,2,1:T(8,128)(2,1)} %bitcast.307, bf16[1024,12,64]{0,2,1:T(8,128)(2,1)} %bitcast.294, f32[12,256,1024]{2,1,0:T(8,128)} %get-tuple-element.245, f32[12,256]{1,0:T(8,128)S(1)} %copy-done.64), kind=kOutput, calls=%fused_computation.209 | convolution fusion | flops 418118656 | bytes 28209152 | tf_op jit(solution)/shard_map/qhd,khd->hqk/dot_general | solution.py:236
  653.4 7.8 slice.78
  661.2 5.3 all-gather.1
  667.0 3.2 fusion.63
  670.3 5.2 multiply_convert_fusion
  677.4 2.9 convolution_bitcast_fusion
  680.3 5.8 copy.122
  686.1 9.1 copy.102
  698.6 6.1 fusion.62
  704.7 4.7 fusion.140
  709.5 4.0 fusion.93
  720.1 4.1 constant_dynamic-update-slice_fusion.3
  727.1 4.4 constant_dynamic-update-slice_fusion.1
  731.5 8.6 constant_dynamic-update-slice_fusion
  740.7 26.1 %gather_fusion.1 = f32[448,128,128]{2,1,0:T(8,128)} fusion(f32[433,128,128]{2,1,0:T(8,128)} %broadcast_dynamic-update-slice_fusion, s32[1024]{0:T(1024)S(1)} %copy-done.46), kind=kCustom, calls=%fused_computation.1 | custom fusion | bytes 58722048 | tf_op jit(solution)/shard_map/gather | solution.py:106
  767.6 5.4 psum.14
  774.4 6.3 fusion.64
  780.6 47.8 %psum.15 = f32[2,768]{1,0:T(2,128)S(1)} all-reduce(f32[2,768]{1,0:T(2,128)S(1)} %pad_maximum_fusion.15), channel_id=1, replica_groups=mesh['dp'=8,'seq'=4] {'dp','seq'}, use_global_device_ids=true, to_apply=%region_26.27 | all-reduce | flops 1536 | bytes 12288 | tf_op jit(solution)/shard_map/psum | solution.py:283
  829.1 2.4 add_bitcast_fusion
  831.5 250.9 %reduce-scatter.8.cloned.1.call-done = f32[14,128,128]{2,1,0:T(8,128)} async-done(((f32[448,128,128]{2,1,0:T(8,128)}), f32[14,128,128]{2,1,0:T(8,128)}) %reduce-scatter.8.cloned.1.call-update) | async-done | bytes 917520 | tf_op jit(solution)/shard_map/reduce_scatter | solution.py:277
  1082.4 3.1 fusion.141
  1085.5 2.8 fusion.79
  1089.8 3.0 fusion.53
  (247 shorter events, 55.1 us)
Async XLA Ops:
  7.2 1078.3 %copy-start = (f32[14,128,128]{2,1,0:T(8,128)S(1)}, f32[14,128,128]{2,1,0:T(8,128)}, u32[]{:S(2)}) copy-start(f32[14,128,128]{2,1,0:T(8,128)} %param.30) | copy-start | bytes 2752516
  7.2 554.0 %all-gather.7.cloned.1.call-start = ((), (), s32[]{:S(2)}) async-start(), calls=%async_computation.4 | async-start | bytes 1966080 | tf_op jit(solution)/shard_map/all_gather | solution.py:178
  8.7 1.9 collective-permute-start
  12.0 23.0 %collective-permute-start.1 = (bf16[2,14,128,128]{3,2,1,0:T(8,128)(2,1)}, bf16[2,14,128,128]{3,2,1,0:T(8,128)(2,1)S(1)}, u32[]{:S(2)}, u32[]{:S(2)}) collective-permute-start(bf16[2,14,128,128]{3,2,1,0:T(8,128)(2,1)} %get-tuple-element.236), channel_id=1, source_target_pairs={{0,2},{1,3},{2,0},{3,1},{4,6},{5,7},{6,4},{7,5},{8,10},{9,11},{10,... | collective-permute-start | bytes 2752520 | tf_op jit(solution)/shard_map/ppermute | solution.py:39
  35.7 40.8 %collective-permute-start.2 = (bf16[4,14,128,128]{3,2,1,0:T(8,128)(2,1)S(1)}, bf16[4,14,128,128]{3,2,1,0:T(8,128)(2,1)}, u32[]{:S(2)}, u32[]{:S(2)}) collective-permute-start(bf16[4,14,128,128]{3,2,1,0:T(8,128)(2,1)S(1)} %bitcast.268), channel_id=1, source_target_pairs={{0,4},{1,5},{2,6},{3,7},{4,0},{5,1},{6,2},{7,3},{8,12},{9,13},{10,... | collective-permute-start | bytes 5505032 | tf_op jit(solution)/shard_map/ppermute | solution.py:39
  81.2 79.4 %collective-permute-start.3 = (bf16[8,14,128,128]{3,2,1,0:T(8,128)(2,1)}, bf16[8,14,128,128]{3,2,1,0:T(8,128)(2,1)}, u32[]{:S(2)}, u32[]{:S(2)}) collective-permute-start(bf16[8,14,128,128]{3,2,1,0:T(8,128)(2,1)} %bitcast.12), channel_id=1, source_target_pairs={{0,8},{1,9},{2,10},{3,11},{4,12},{5,13},{6,14},{7,15},{8,0},{9,1},... | collective-permute-start | bytes 11010056 | tf_op jit(solution)/shard_map/ppermute | solution.py:39
  164.4 7.8 copy-start.52
  164.4 8.6 copy-start.37
  164.4 8.6 copy-start.7
  170.7 318.2 %collective-permute-start.4 = (bf16[16,14,128,128]{3,2,1,0:T(8,128)(2,1)}, bf16[16,14,128,128]{3,2,1,0:T(8,128)(2,1)}, u32[]{:S(2)}, u32[]{:S(2)}) collective-permute-start(bf16[16,14,128,128]{3,2,1,0:T(8,128)(2,1)} %bitcast.15), channel_id=1, source_target_pairs={{0,16},{1,17},{2,18},{3,19},{4,20},{5,21},{6,22},{7,23},{8,24},{9,... | collective-permute-start | bytes 22020104 | tf_op jit(solution)/shard_map/ppermute | solution.py:39
  173.2 353.5 %copy-start.42 = (f32[256]{0:T(256)}, f32[256]{0:T(256)S(1)}, u32[]{:S(2)}) copy-start(f32[256]{0:T(256)S(1)} %broadcast_multiply_fusion.2) | copy-start | bytes 3076
  173.4 323.0 %copy-start.47 = (f32[256]{0:T(256)}, f32[256]{0:T(256)S(1)}, u32[]{:S(2)}) copy-start(f32[256]{0:T(256)S(1)} %fusion.92) | copy-start | bytes 3076
  173.5 353.2 %copy-start.44 = (f32[256]{0:T(256)}, f32[256]{0:T(256)S(1)}, u32[]{:S(2)}) copy-start(f32[256]{0:T(256)S(1)} %fusion.114) | copy-start | bytes 3076
  529.8 68.0 %all-gather.5.cloned.1.call-start = ((), (), s32[]{:S(2)}) async-start(), calls=%async_computation.3 | async-start | bytes 1966080 | tf_op jit(solution)/shard_map/all_gather | solution.py:179
  532.2 30.7 %copy-start.28 = (bf16[256,768]{0,1:T(8,128)(2,1)}, bf16[256,768]{0,1:T(8,128)(2,1)S(1)}, u32[]{:S(2)}) copy-start(bf16[256,768]{0,1:T(8,128)(2,1)S(1)} %copy.91) | copy-start | bytes 1179652
  561.1 148.3 %reduce-scatter.6.cloned.1.call-start = ((), (), s32[]{:S(2)}) async-start(), calls=%async_computation.6 | async-start | bytes 1966080 | tf_op jit(solution)/shard_map/reduce_scatter | solution.py:264
  563.0 6.5 copy-start.40
  563.0 6.5 copy-start.50
  563.0 6.4 copy-start.56
  563.0 6.4 copy-start.59
  570.7 9.0 copy-start.30
  597.8 12.4 %copy-start.63 = (f32[12,256]{1,0:T(8,128)}, f32[12,256]{1,0:T(8,128)S(1)}, u32[]{:S(2)}) copy-start(f32[12,256]{1,0:T(8,128)S(1)} %get-tuple-element.244) | copy-start | bytes 36868
  599.5 10.7 copy-start.26
  599.5 12.4 %slice-start.7 = ((s8[4718592]{0:T(1024)(128)(4,1)}), s8[4194304]{0:T(1024)(128)(4,1)S(1)}, s32[]{:S(2)}) async-start(s8[4718592]{0:T(1024)(128)(4,1)} %bitcast.279), calls=%async_computation.15 | async-start | bytes 8388608
  599.5 11.6 %copy-start.11 = (bf16[6,128,6,128]{3,2,1,0:T(8,128)(2,1)S(1)}, bf16[6,128,6,128]{3,2,1,0:T(8,128)(2,1)}, u32[]{:S(2)}) copy-start(bf16[6,128,6,128]{3,2,1,0:T(8,128)(2,1)} %copy.93) | copy-start | bytes 3538948
  599.5 12.4 %slice-start.8 = ((s8[4718592]{0:T(1024)(128)(4,1)}), s8[524288]{0:T(1024)(128)(4,1)S(1)}, s32[]{:S(2)}) async-start(s8[4718592]{0:T(1024)(128)(4,1)} %bitcast.279), calls=%async_computation.16 | async-start | bytes 1048576
  611.7 65.7 %copy-start.4 = (f32[256,768]{1,0:T(8,128)}, f32[256,768]{1,0:T(8,128)S(1)}, u32[]{:S(2)}) copy-start(f32[256,768]{1,0:T(8,128)S(1)} %get-tuple-element.247) | copy-start | bytes 2359300
  630.3 11.4 %copy-start.34 = (bf16[256,768]{0,1:T(8,128)(2,1)}, bf16[256,768]{0,1:T(8,128)(2,1)S(1)}, u32[]{:S(2)}) copy-start(bf16[256,768]{0,1:T(8,128)(2,1)S(1)} %copy.97) | copy-start | bytes 1179652
  630.3 11.5 %copy-start.20 = (f32[256,768]{1,0:T(8,128)S(1)}, f32[256,768]{1,0:T(8,128)}, u32[]{:S(2)}) copy-start(f32[256,768]{1,0:T(8,128)} %get-tuple-element.249) | copy-start | bytes 2359300
  641.7 67.8 %reduce-scatter.4.cloned.1.call-start = ((), (), s32[]{:S(2)}) async-start(), calls=%async_computation.5 | async-start | bytes 1966080 | tf_op jit(solution)/shard_map/reduce_scatter | solution.py:258
  653.4 13.5 %copy-start.41 = (s32[1,1024]{1,0:T(1,128)S(1)}, s32[1,1024]{1,0:T(1,128)}, u32[]{:S(2)}) copy-start(s32[1,1024]{1,0:T(1,128)} %param.19) | copy-start | bytes 12292
  653.4 13.5 %copy-start.51 = (s32[1,256]{1,0:T(1,128)S(1)}, s32[1,256]{1,0:T(1,128)}, u32[]{:S(2)}) copy-start(s32[1,256]{1,0:T(1,128)} %copy-done.49) | copy-start | bytes 3076
  653.4 13.5 %copy-start.57 = (s32[256]{0:T(256)S(1)}, s32[256]{0:T(256)}, u32[]{:S(2)}) copy-start(s32[256]{0:T(256)} %copy-done.55) | copy-start | bytes 3076
  653.4 13.5 %copy-start.60 = (pred[1024]{0:T(1024)(128)(4,1)S(1)}, pred[1024]{0:T(1024)(128)(4,1)}, u32[]{:S(2)}) copy-start(pred[1024]{0:T(1024)(128)(4,1)} %copy-done.58) | copy-start | bytes 3076
  661.2 9.0 copy-start.29
  675.4 407.0 %reduce-scatter.8.cloned.1.call-start = ((), (), s32[]{:S(2)}) async-start(), calls=%async_computation.7 | async-start | bytes 30277632 | tf_op jit(solution)/shard_map/reduce_scatter | solution.py:277
  686.1 9.1 copy-start.25
  720.1 6.9 slice-start.3
  720.1 7.1 slice-start.4
  731.5 9.2 copy-start.46
  766.8 7.5 copy-start.5
  774.3 54.1 %copy-start.38 = (f32[2,768]{1,0:T(2,128)S(1)}, f32[2,768]{1,0:T(2,128)}, u32[]{:S(2)}) copy-start(f32[2,768]{1,0:T(2,128)} %param.22) | copy-start | bytes 18436
  774.3 54.1 %copy-start.53 = (f32[2,768]{1,0:T(2,128)S(1)}, f32[2,768]{1,0:T(2,128)}, u32[]{:S(2)}) copy-start(f32[2,768]{1,0:T(2,128)} %param.23) | copy-start | bytes 18436
  774.3 54.1 %copy-start.54 = (f32[2,768]{1,0:T(2,128)S(1)}, f32[2,768]{1,0:T(2,128)}, u32[]{:S(2)}) copy-start(f32[2,768]{1,0:T(2,128)} %param.24) | copy-start | bytes 18436
  774.3 54.8 %copy-start.3 = (f32[256,768]{1,0:T(8,128)S(1)}, f32[256,768]{1,0:T(8,128)}, u32[]{:S(2)}) copy-start(f32[256,768]{1,0:T(8,128)} %copy-done.2) | copy-start | bytes 2359300
  774.3 54.7 %copy-start.9 = (bf16[1,256,768]{2,1,0:T(8,128)(2,1)S(1)}, bf16[1,256,768]{2,1,0:T(8,128)(2,1)}, u32[]{:S(2)}) copy-start(bf16[1,256,768]{2,1,0:T(8,128)(2,1)} %param.18) | copy-start | bytes 1179652
  774.4 54.7 %copy-start.19 = (bf16[1,256,768]{2,1,0:T(8,128)(2,1)S(1)}, bf16[1,256,768]{2,1,0:T(8,128)(2,1)}, u32[]{:S(2)}) copy-start(bf16[1,256,768]{2,1,0:T(8,128)(2,1)} %param.31) | copy-start | bytes 1179652
  831.5 256.8 %copy-start.31 = (f32[14,128,128]{2,1,0:T(8,128)S(1)}, f32[14,128,128]{2,1,0:T(8,128)}, u32[]{:S(2)}) copy-start(f32[14,128,128]{2,1,0:T(8,128)} %param.29) | copy-start | bytes 2752516
  (36 other events, 128.9 us)
Sparse Core Ops, SparseCore 0:
  529.9 20.4 all-gather.6
  561.3 20.4 all-gather.4
  641.8 27.8 reduce-scatter.5
  675.6 27.7 reduce-scatter.3
  767.0 315.4 reduce-scatter.7
